TPU v7x, 32 devices: a whole 2x2x4 slice. The times are simulated.
32 devices in a mesh: groups: 2 (over y), ctx: 4 (over z), head: 2 (over x), rows: 2 (over core).
Axes of the slice: x: 2, y: 2, z: 4, core: 2. Of those that a mesh axis runs over, the one named last changes fastest.
Arguments:
- keys: bfloat16 [65536, 1024], P(('groups', 'ctx'), 'head'), parts along dimension 0, may hold values from -18 to 18
- values: bfloat16 [65536, 1024], P(('groups', 'ctx'), 'head'), parts along dimension 0, may hold values from -6 to 6
- window_q: bfloat16 [64, 8192], P(('groups', 'ctx'), 'head'), parts along dimension 0, may hold values from -6 to 6
- keep_stretches: int32 [16, 20], P(('groups', 'head')), parts along dimension 0, may hold values from 0 to 62, as said below
- dec_q: bfloat16 [128, 4, 8192], P('groups', None, 'head'), parts along dimension 0, may hold values from -6 to 6
- dec_k: bfloat16 [128, 4, 1024], P('groups', None, 'head'), parts along dimension 0, may hold values from -8 to 8
- dec_v: bfloat16 [128, 4, 1024], P('groups', None, 'head'), parts along dimension 0, may hold values from -6 to 6
- row_order: int32 [128], P('groups'), parts along dimension 0, may hold values from 0 to 63, each once
Outputs:
- stretch_scores: float32 [16, 64], P(('groups', 'head', 'rows'), 'ctx'), parts along dimension 0
- decoded: bfloat16 [128, 4, 8192], P(('groups', 'ctx', 'rows'), None, 'head'), parts along dimension 0
There are 2 independent parts, one for each index of `groups`. A program takes and returns all parts, laid end to end along the dimension named above; each array names one. Nothing has to cross between parts.
Inputs may be any that keep to these rules, and one draw needn't show every extreme that they name: keep_stretches[k] lists 20 distinct stretch numbers of key-value head k in ascending order and never the last stretch; for every head some context shard has all 16 of its stretches listed.
All inputs are finite; a program needn't handle non-finite values.
Results may differ from a plain program's by a relative error of at most 0.0045.
Values may be sent and summed in bfloat16 or wider, within the bound.
No kernel may reach another device: no remote copies, remote signals or barrier semaphores. Data moves between devices by JAX's collectives and lax.ppermute only.
A program may use at most 128 MiB of HBM per device.

v0:
```python
import math

import jax
import jax.numpy as jnp
from jax import lax
from jax.sharding import PartitionSpec as P

QH = 64
KVH = 8
HD = 128
STRETCH = 512
W = 32


MASK_FILL = -1e30


def merged(x, axis, combine):
    everything = jax.tree.map(lambda part: lax.all_gather(part, axis), x)
    first = jax.tree.map(lambda part: part[0], everything)

    def step(k, so_far):
        return combine(so_far, jax.tree.map(lambda part: part[k], everything))

    return lax.fori_loop(1, lax.axis_size(axis), step, first)


def combine_soft(left_part, right_part):
    maxima = jnp.maximum(left_part[0], right_part[0])
    left_scale = jnp.exp(left_part[0] - maxima)
    right_scale = jnp.exp(right_part[0] - maxima)
    totals = left_part[1] * left_scale + right_part[1] * right_scale
    if len(left_part) == 2:
        return (maxima, totals)
    weighted = left_part[2] * left_scale[..., None] + right_part[2] * right_scale[..., None]
    return (maxima, totals, weighted)


def fold_keys(queries, key_blocks, value_blocks, mask_blocks, score_scale):
    score_form = "qghd,kgd->qghk"
    value_form = "qghk,kgd->qghd"
    count, heads, group_size, depth = queries.shape
    start_state = (
        jnp.full((count, heads, group_size), MASK_FILL, jnp.float32),
        jnp.zeros((count, heads, group_size), jnp.float32),
        jnp.zeros((count, heads, group_size, depth), jnp.float32),
    )

    def advance(state_now, block_data):
        key_block, value_block, mask_block = block_data
        valid_mask = mask_block[None, :, None, :]
        scores = (
            jnp.einsum(score_form, queries, key_block, preferred_element_type=jnp.float32)
            * score_scale
        )
        scores = jnp.where(valid_mask, scores, MASK_FILL)
        maxima = jnp.maximum(state_now[0], jnp.max(scores, axis=3))
        weights = jnp.where(valid_mask, jnp.exp(scores - maxima[..., None]), 0.0)
        shrink = jnp.exp(state_now[0] - maxima)
        totals = state_now[1] * shrink + jnp.sum(weights, axis=3)
        weighted = state_now[2] * shrink[..., None] + jnp.einsum(
            value_form,
            weights.astype(jnp.bfloat16),
            value_block,
            preferred_element_type=jnp.float32,
        )
        return ((maxima, totals, weighted), None)

    result, unused = lax.scan(advance, start_state, (key_blocks, value_blocks, mask_blocks))
    return result


def local(keys, values, window_q, keep_stretches, dec_q, dec_k, dec_v, row_order):
    ctx_count = lax.axis_size("ctx")
    row_count = lax.axis_size("rows")
    own_index = lax.axis_index("ctx")
    row_index = lax.axis_index("rows")
    ctx_dev = keys.shape[0]
    local_heads = keys.shape[1] // HD
    group_size = QH // KVH
    score_scale = HD ** (-0.5)
    stretches_here = ctx_dev // STRETCH
    total_ctx = ctx_dev * ctx_count
    is_last = own_index == ctx_count - 1
    key_heads = keys.reshape(ctx_dev, local_heads, HD)
    value_heads = values.reshape(ctx_dev, local_heads, HD)
    score_heads = local_heads // row_count
    query_cols = score_heads * group_size * HD
    mine_query = lax.dynamic_slice_in_dim(window_q, row_index * query_cols, query_cols, 1)
    whole_query = lax.all_gather(mine_query, "ctx", axis=0, tiled=True)
    window_query = whole_query.reshape(W, score_heads, group_size, HD)
    scored_keys = lax.dynamic_slice_in_dim(key_heads, row_index * score_heads, score_heads, 1)
    scores = (
        jnp.einsum("wghd,tgd->gwht", window_query, scored_keys, preferred_element_type=jnp.float32)
        * score_scale
    )
    positions = own_index * ctx_dev + jnp.arange(ctx_dev, dtype=jnp.int32)
    reaches = total_ctx - W + jnp.arange(W, dtype=jnp.int32)
    allowed = (positions[None, :] <= reaches[:, None])[None, :, None, :]
    masked = jnp.where(allowed, scores, MASK_FILL)
    maxima = jnp.max(masked, axis=3)
    totals = jnp.sum(jnp.where(allowed, jnp.exp(masked - maxima[..., None]), 0.0), axis=3)
    maxima, totals = merged((maxima, totals), "ctx", combine_soft)
    probability = jnp.where(allowed, jnp.exp(masked - maxima[..., None]), 0.0) / totals[..., None]
    stretch_scores = (
        jnp.sum(probability, axis=(1, 2)).reshape(score_heads, stretches_here, STRETCH).sum(axis=2)
    )
    rows_each = dec_q.shape[0] // (ctx_count * row_count)
    step_count = dec_q.shape[1]
    slot_ids = (
        jnp.arange(ctx_count, dtype=jnp.int32)[:, None] * (row_count * rows_each)
        + row_index * rows_each
        + jnp.arange(rows_each, dtype=jnp.int32)[None, :]
    ).reshape(-1)
    chosen = row_order[slot_ids]
    local_rows = ctx_count * rows_each
    queries = dec_q[chosen].reshape(local_rows * step_count, local_heads, group_size, HD)
    own_keys = dec_k[chosen].reshape(local_rows, step_count, local_heads, HD)
    own_values = dec_v[chosen].reshape(local_rows, step_count, local_heads, HD)
    stretch_base = own_index * stretches_here + jnp.arange(stretches_here, dtype=jnp.int32)
    kept_flag = (
        jnp.sum(
            (keep_stretches[:, :, None] == stretch_base[None, None, :]).astype(jnp.int32), axis=1
        )
        > 0
    )
    per_block = math.gcd(stretches_here, max(1, 2048 // STRETCH))
    block_count = stretches_here // per_block
    block_len = per_block * STRETCH
    valid_mask = jnp.broadcast_to(
        kept_flag.reshape(local_heads, block_count, per_block, 1),
        (local_heads, block_count, per_block, STRETCH),
    )
    valid_mask = valid_mask.reshape(local_heads, block_count, block_len).transpose(1, 0, 2)
    kept_part = fold_keys(
        queries,
        key_heads.reshape(block_count, block_len, local_heads, HD),
        value_heads.reshape(block_count, block_len, local_heads, HD),
        valid_mask,
        score_scale,
    )
    window_mask = jnp.broadcast_to(is_last, (1, local_heads, W))
    window_part = fold_keys(
        queries,
        key_heads[ctx_dev - W :].reshape(1, W, local_heads, HD),
        value_heads[ctx_dev - W :].reshape(1, W, local_heads, HD),
        window_mask,
        score_scale,
    )
    own_query = queries.reshape(local_rows, step_count, local_heads, group_size, HD)
    own_scores = (
        jnp.einsum("rsghd,rtgd->rsght", own_query, own_keys, preferred_element_type=jnp.float32)
        * score_scale
    )
    causal = (
        jnp.arange(step_count, dtype=jnp.int32)[None, :]
        <= jnp.arange(step_count, dtype=jnp.int32)[:, None]
    )[None, :, None, None, :] & is_last
    own_masked = jnp.where(causal, own_scores, MASK_FILL)
    own_max = jnp.max(own_masked, axis=4)
    own_weights = jnp.where(causal, jnp.exp(own_masked - own_max[..., None]), 0.0)
    own_totals = jnp.sum(own_weights, axis=4)
    own_weighted = jnp.einsum(
        "rsght,rtgd->rsghd",
        own_weights.astype(jnp.bfloat16),
        own_values,
        preferred_element_type=jnp.float32,
    )
    query_count = local_rows * step_count
    own_part = (
        own_max.reshape(query_count, local_heads, group_size),
        own_totals.reshape(query_count, local_heads, group_size),
        own_weighted.reshape(query_count, local_heads, group_size, HD),
    )
    partial_value = combine_soft(kept_part, window_part)
    partial_value = combine_soft(partial_value, own_part)
    maxima = lax.pmax(partial_value[0], "ctx")
    shrink = jnp.exp(partial_value[0] - maxima)
    weighted, totals = (
        lax.psum_scatter(
            partial_value[2] * shrink[..., None], "ctx", scatter_dimension=0, tiled=True
        ),
        lax.psum_scatter(partial_value[1] * shrink, "ctx", scatter_dimension=0, tiled=True),
    )
    decoded = (
        (weighted / totals[..., None])
        .reshape(rows_each, step_count, local_heads * group_size * HD)
        .astype(jnp.bfloat16)
    )
    return (stretch_scores, decoded)


def solution(mesh):
    placed = (
        P(("groups", "ctx"), "head"),
        P(("groups", "ctx"), "head"),
        P(("groups", "ctx"), "head"),
        P(("groups", "head"), None),
        P("groups", None, "head"),
        P("groups", None, "head"),
        P("groups", None, "head"),
        P("groups"),
    )
    return jax.shard_map(
        local,
        mesh=mesh,
        in_specs=placed,
        out_specs=(
            P(("groups", "head", "rows"), "ctx"),
            P(("groups", "ctx", "rows"), None, "head"),
        ),
        check_vma=False,
    )
```

profile of v0, /device:TPU:0, one launch (start us, length us, event | category | flops | bytes accessed | tf_op | source)
XLA Modules:
  0.0 380.2 jit_solution(2156224945438028613)
XLA Ops:
  7.4 1.5 gather_fusion
  8.9 1.4 gather_fusion.1
  10.4 1.9 reshape_reshape.11
  12.3 1.1 reshape.181
  13.4 12.6 %reshape_reshape.9 = bf16[4,2048,4,128]{3,2,1,0:T(4,128)(2,1)} reshape(bf16[8192,512]{1,0:T(8,128)(2,1)} %param.12) | data formatting | bytes 16777216 | tf_op jit(solution)/shard_map/reshape;reshape | solution.py:137
  26.8 5.8 %fusion.60 = (f32[32,4,4,8]{3,1,2,0:T(4,128)S(1)}, f32[32,4,4,8,4]{3,4,1,2,0:T(4,128)}) fusion(bf16[32,4,4,8,128]{4,3,2,1,0:T(8,128)(2,1)S(1)} %copy-done.6, bf16[32,4,512]{2,1,0:T(4,128)(2,1)S(1)} %gather_fusion.2, pred[4,4]{1,0:T(4,128)(4,1)S(1)} %fusion.50), kind=kOutput, calls=%fused_computation.105 | convolution fusion | flops 4239360 | bytes 1261584 | tf_op jit(solution)/shard_map/rsghd,rtgd->rsght/dot_general | solution.py:152
  33.8 1.9 fusion.61
  36.2 12.5 %reshape_reshape.10 = bf16[4,2048,4,128]{3,2,1,0:T(4,128)(2,1)} reshape(bf16[8192,512]{1,0:T(8,128)(2,1)} %param.13) | data formatting | bytes 16777216 | tf_op jit(solution)/shard_map/reshape;reshape | solution.py:138
  48.7 199.0 %while.39 = (s32[]{:T(128)}, f32[128,4,8]{0,2,1:T(8,128)S(1)}, f32[128,4,8]{0,2,1:T(8,128)S(1)}, f32[128,4,8,128]{0,3,2,1:T(8,128)}, pred[4,4,2048]{2,1,0:T(4,12...) while((s32[]{:T(128)}, f32[128,4,8]{0,2,1:T(8,128)S(1)}, ...), condition=%wide.region_10.11_spmd.clone, body=%wide.region_7.10_spmd.clone.sunk | while | flops 4405612544 | bytes 131375248 | solution.py:69
  48.7 4.1 %constant_dynamic-slice_fusion.4 = (bf16[1,2048,4,128]{3,2,1,0:T(4,128)(2,1)}, bf16[1,2048,4,128]{3,2,1,0:T(4,128)(2,1)S(1)}) fusion(bf16[4,2048,4,128]{3,2,1,0:T(4,128)(2,1)} %get-tuple-element.463, s32[]{:T(128)} %get-tuple-element.446, bf16[4,2048,4,128]{3,2,1,0:T(4,128)(2,1)} %get-tuple-element.461), kind=kLoop, calls=%fused_computation.29.clone.1 | loop fusion | bytes 8388612 | tf_op jit(solution)/shard_map/while/body/jit(dynamic_index_in_dim)/dynamic_slice | solution.py:69
  52.8 12.1 %bitcast_reduce_fusion.3 = (f32[128,4,8]{0,2,1:T(8,128)S(1)}, f32[4,2048,128,8]{2,1,3,0:T(8,128)}) fusion(pred[4,2048]{1,0:T(4,128)(4,1)S(1)} %dynamic-slice_bitcast_fusion.2, bf16[128,4,8,128]{3,0,2,1:T(8,128)(2,1)S(1)} %get-tuple-element.462, bf16[1,2048,4,128]{3,2,1,0:T(4,128)(2,1)S(1)} %get-tuple-element.406), kind=kOutput, calls=%fused_computation.10.clone.1 | convolution fusion | flops 2172645376 | bytes 36724736 | tf_op jit(solution)/shard_map/while/body/eval_jaxpr/qghd,kgd->qghk/dot_general | solution.py:53
  64.9 15.3 %fusion.73 = f32[128,4,8]{0,2,1:T(8,128)S(1)} fusion(f32[4,2048,128,8]{2,1,3,0:T(8,128)} %get-tuple-element.408, f32[128,4,8]{0,2,1:T(8,128)S(1)} %select_maximum_fusion.2, pred[4,2048]{1,0:T(4,128)(4,1)S(1)} %dynamic-slice_bitcast_fusion.2), kind=kLoop, calls=%fused_computation.15.clone.1 | loop fusion | flops 41938944 | bytes 33595392 | tf_op jit(solution)/shard_map/while/body/eval_jaxpr/reduce_sum | solution.py:60
  80.3 2.7 copy.178
  82.9 15.5 %bitcast_add_fusion.3 = f32[128,4,8,128]{0,3,2,1:T(8,128)} fusion(f32[128,4,8,128]{0,3,2,1:T(8,128)} %get-tuple-element.449, f32[4,2048,128,8]{2,1,3,0:T(8,128)} %get-tuple-element.408, f32[128,4,8]{0,2,1:T(8,128)S(1)} %select_maximum_fusion.2, pred[4,2048]{1,0:T(4,128)(4,1)S(1)} %dynamic-slice_bitcast_fusion.2, ...), kind=kOutput, calls=%fused_computation.22.clone.1 | convolution fusion | flops 2190999552 | bytes 39886848 | tf_op jit(solution)/shard_map/while/body/eval_jaxpr/qghk,kgd->qghd/dot_general | solution.py:61
  98.4 4.0 %constant_dynamic-slice_fusion.4 = (bf16[1,2048,4,128]{3,2,1,0:T(4,128)(2,1)}, bf16[1,2048,4,128]{3,2,1,0:T(4,128)(2,1)S(1)}) fusion(bf16[4,2048,4,128]{3,2,1,0:T(4,128)(2,1)} %get-tuple-element.463, s32[]{:T(128)} %get-tuple-element.446, bf16[4,2048,4,128]{3,2,1,0:T(4,128)(2,1)} %get-tuple-element.461), kind=kLoop, calls=%fused_computation.29.clone.1 | loop fusion | bytes 8388612 | tf_op jit(solution)/shard_map/while/body/jit(dynamic_index_in_dim)/dynamic_slice | solution.py:69
  102.4 12.1 %bitcast_reduce_fusion.3 = (f32[128,4,8]{0,2,1:T(8,128)S(1)}, f32[4,2048,128,8]{2,1,3,0:T(8,128)}) fusion(pred[4,2048]{1,0:T(4,128)(4,1)S(1)} %dynamic-slice_bitcast_fusion.2, bf16[128,4,8,128]{3,0,2,1:T(8,128)(2,1)S(1)} %get-tuple-element.462, bf16[1,2048,4,128]{3,2,1,0:T(4,128)(2,1)S(1)} %get-tuple-element.406), kind=kOutput, calls=%fused_computation.10.clone.1 | convolution fusion | flops 2172645376 | bytes 36724736 | tf_op jit(solution)/shard_map/while/body/eval_jaxpr/qghd,kgd->qghk/dot_general | solution.py:53
  114.6 15.3 %fusion.73 = f32[128,4,8]{0,2,1:T(8,128)S(1)} fusion(f32[4,2048,128,8]{2,1,3,0:T(8,128)} %get-tuple-element.408, f32[128,4,8]{0,2,1:T(8,128)S(1)} %select_maximum_fusion.2, pred[4,2048]{1,0:T(4,128)(4,1)S(1)} %dynamic-slice_bitcast_fusion.2), kind=kLoop, calls=%fused_computation.15.clone.1 | loop fusion | flops 41938944 | bytes 33595392 | tf_op jit(solution)/shard_map/while/body/eval_jaxpr/reduce_sum | solution.py:60
  129.9 2.7 copy.178
  132.5 15.6 %bitcast_add_fusion.3 = f32[128,4,8,128]{0,3,2,1:T(8,128)} fusion(f32[128,4,8,128]{0,3,2,1:T(8,128)} %get-tuple-element.449, f32[4,2048,128,8]{2,1,3,0:T(8,128)} %get-tuple-element.408, f32[128,4,8]{0,2,1:T(8,128)S(1)} %select_maximum_fusion.2, pred[4,2048]{1,0:T(4,128)(4,1)S(1)} %dynamic-slice_bitcast_fusion.2, ...), kind=kOutput, calls=%fused_computation.22.clone.1 | convolution fusion | flops 2190999552 | bytes 39886848 | tf_op jit(solution)/shard_map/while/body/eval_jaxpr/qghk,kgd->qghd/dot_general | solution.py:61
  148.2 4.0 %constant_dynamic-slice_fusion.4 = (bf16[1,2048,4,128]{3,2,1,0:T(4,128)(2,1)}, bf16[1,2048,4,128]{3,2,1,0:T(4,128)(2,1)S(1)}) fusion(bf16[4,2048,4,128]{3,2,1,0:T(4,128)(2,1)} %get-tuple-element.463, s32[]{:T(128)} %get-tuple-element.446, bf16[4,2048,4,128]{3,2,1,0:T(4,128)(2,1)} %get-tuple-element.461), kind=kLoop, calls=%fused_computation.29.clone.1 | loop fusion | bytes 8388612 | tf_op jit(solution)/shard_map/while/body/jit(dynamic_index_in_dim)/dynamic_slice | solution.py:69
  152.2 12.1 %bitcast_reduce_fusion.3 = (f32[128,4,8]{0,2,1:T(8,128)S(1)}, f32[4,2048,128,8]{2,1,3,0:T(8,128)}) fusion(pred[4,2048]{1,0:T(4,128)(4,1)S(1)} %dynamic-slice_bitcast_fusion.2, bf16[128,4,8,128]{3,0,2,1:T(8,128)(2,1)S(1)} %get-tuple-element.462, bf16[1,2048,4,128]{3,2,1,0:T(4,128)(2,1)S(1)} %get-tuple-element.406), kind=kOutput, calls=%fused_computation.10.clone.1 | convolution fusion | flops 2172645376 | bytes 36724736 | tf_op jit(solution)/shard_map/while/body/eval_jaxpr/qghd,kgd->qghk/dot_general | solution.py:53
  164.3 15.3 %fusion.73 = f32[128,4,8]{0,2,1:T(8,128)S(1)} fusion(f32[4,2048,128,8]{2,1,3,0:T(8,128)} %get-tuple-element.408, f32[128,4,8]{0,2,1:T(8,128)S(1)} %select_maximum_fusion.2, pred[4,2048]{1,0:T(4,128)(4,1)S(1)} %dynamic-slice_bitcast_fusion.2), kind=kLoop, calls=%fused_computation.15.clone.1 | loop fusion | flops 41938944 | bytes 33595392 | tf_op jit(solution)/shard_map/while/body/eval_jaxpr/reduce_sum | solution.py:60
  179.7 2.7 copy.178
  182.3 15.6 %bitcast_add_fusion.3 = f32[128,4,8,128]{0,3,2,1:T(8,128)} fusion(f32[128,4,8,128]{0,3,2,1:T(8,128)} %get-tuple-element.449, f32[4,2048,128,8]{2,1,3,0:T(8,128)} %get-tuple-element.408, f32[128,4,8]{0,2,1:T(8,128)S(1)} %select_maximum_fusion.2, pred[4,2048]{1,0:T(4,128)(4,1)S(1)} %dynamic-slice_bitcast_fusion.2, ...), kind=kOutput, calls=%fused_computation.22.clone.1 | convolution fusion | flops 2190999552 | bytes 39886848 | tf_op jit(solution)/shard_map/while/body/eval_jaxpr/qghk,kgd->qghd/dot_general | solution.py:61
  198.0 4.0 %constant_dynamic-slice_fusion.4 = (bf16[1,2048,4,128]{3,2,1,0:T(4,128)(2,1)}, bf16[1,2048,4,128]{3,2,1,0:T(4,128)(2,1)S(1)}) fusion(bf16[4,2048,4,128]{3,2,1,0:T(4,128)(2,1)} %get-tuple-element.463, s32[]{:T(128)} %get-tuple-element.446, bf16[4,2048,4,128]{3,2,1,0:T(4,128)(2,1)} %get-tuple-element.461), kind=kLoop, calls=%fused_computation.29.clone.1 | loop fusion | bytes 8388612 | tf_op jit(solution)/shard_map/while/body/jit(dynamic_index_in_dim)/dynamic_slice | solution.py:69
  202.0 12.1 %bitcast_reduce_fusion.3 = (f32[128,4,8]{0,2,1:T(8,128)S(1)}, f32[4,2048,128,8]{2,1,3,0:T(8,128)}) fusion(pred[4,2048]{1,0:T(4,128)(4,1)S(1)} %dynamic-slice_bitcast_fusion.2, bf16[128,4,8,128]{3,0,2,1:T(8,128)(2,1)S(1)} %get-tuple-element.462, bf16[1,2048,4,128]{3,2,1,0:T(4,128)(2,1)S(1)} %get-tuple-element.406), kind=kOutput, calls=%fused_computation.10.clone.1 | convolution fusion | flops 2172645376 | bytes 36724736 | tf_op jit(solution)/shard_map/while/body/eval_jaxpr/qghd,kgd->qghk/dot_general | solution.py:53
  214.1 15.3 %fusion.73 = f32[128,4,8]{0,2,1:T(8,128)S(1)} fusion(f32[4,2048,128,8]{2,1,3,0:T(8,128)} %get-tuple-element.408, f32[128,4,8]{0,2,1:T(8,128)S(1)} %select_maximum_fusion.2, pred[4,2048]{1,0:T(4,128)(4,1)S(1)} %dynamic-slice_bitcast_fusion.2), kind=kLoop, calls=%fused_computation.15.clone.1 | loop fusion | flops 41938944 | bytes 33595392 | tf_op jit(solution)/shard_map/while/body/eval_jaxpr/reduce_sum | solution.py:60
  229.4 2.7 copy.178
  232.1 15.6 %bitcast_add_fusion.3 = f32[128,4,8,128]{0,3,2,1:T(8,128)} fusion(f32[128,4,8,128]{0,3,2,1:T(8,128)} %get-tuple-element.449, f32[4,2048,128,8]{2,1,3,0:T(8,128)} %get-tuple-element.408, f32[128,4,8]{0,2,1:T(8,128)S(1)} %select_maximum_fusion.2, pred[4,2048]{1,0:T(4,128)(4,1)S(1)} %dynamic-slice_bitcast_fusion.2, ...), kind=kOutput, calls=%fused_computation.22.clone.1 | convolution fusion | flops 2190999552 | bytes 39886848 | tf_op jit(solution)/shard_map/while/body/eval_jaxpr/qghk,kgd->qghd/dot_general | solution.py:61
  247.8 20.6 %pmax.7 = f32[128,4,8]{0,2,1:T(8,128)S(1)} all-reduce(f32[128,4,8]{0,2,1:T(8,128)S(1)} %get-tuple-element.308), channel_id=1, replica_groups=mesh['groups'=2,'ctx'=4,'head'=2,'rows'=2] {'ctx'}, use_global_device_ids=true, to_apply=%region_13.14 | all-reduce | flops 4096 | bytes 32768 | tf_op jit(solution)/shard_map/pmax | solution.py:177
  268.4 2.3 fusion.33
  270.9 1.2 fusion.39
  272.1 0.7 copy.145
  272.9 1.7 gather_fusion.3
  274.6 2.0 convolution_bitcast_fusion
  276.6 2.0 copy.126
  278.6 3.0 copy.119
  281.6 8.1 %fusion.27 = f32[128,4,8,128]{3,0,2,1:T(8,128)} fusion(f32[128,4,8,128]{3,0,2,1:T(8,128)} %bitcast.139, f32[128,4,8,128]{3,0,2,1:T(8,128)} %copy.119, f32[128,4,8]{0,2,1:T(8,128)S(1)} %get-tuple-element.302, f32[128,4,8]{0,2,1:T(8,128)S(1)} %get-tuple-element.301, f32[128,4,8]{0,2,1:T(8,128)S(1)} %get-tuple-element.300, ...), kind=kOutput, calls=%fused_computation.45 | convolution fusion | flops 38141952 | bytes 6963201 | tf_op jit(solution)/shard_map/while/body/eval_jaxpr/qghk,kgd->qghd/dot_general | solution.py:61
  289.7 11.3 %copy.106 = bf16[8192,512]{0,1:T(8,128)(2,1)} copy(bf16[8192,512]{1,0:T(8,128)(2,1)} %param.12) | data formatting | bytes 16777216 | tf_op args[0]
  301.0 14.7 %all_gather.15 = bf16[32,2048]{1,0:T(8,128)(2,1)S(1)} all-gather(bf16[8,2048]{1,0:T(8,128)(2,1)S(1)} %constant_dynamic-slice_fusion.2), channel_id=1, replica_groups=mesh['groups'=2,'ctx'=4,'head'=2,'rows'=2] {'ctx'}, dimensions={0}, use_global_device_ids=true | all-gather | bytes 163840 | tf_op jit(solution)/shard_map/all_gather | solution.py:90
  316.0 10.5 %fusion.59 = (f32[2,32,8]{2,1,0:T(8,128)S(1)}, f32[2,32,8,8192]{3,2,1,0:T(8,128)}) fusion(bf16[8192,4,128]{0,2,1:T(8,128)(2,1)} %bitcast.138, s32[]{:T(128)S(6)} %select_n.79, bf16[32,2,8,128]{3,2,1,0:T(8,128)(2,1)S(1)} %bitcast.142, pred[32,8192]{1,0:T(8,128)(4,1)S(1)} %broadcast_compare_fusion), kind=kOutput, calls=%fused_computation.104 | convolution fusion | flops 1086324224 | bytes 21366788 | tf_op jit(solution)/shard_map/wghd,tgd->gwht/dot_general | solution.py:94
  326.6 8.2 %select_reduce_fusion = f32[2,32,8]{2,1,0:T(8,128)S(1)} fusion(f32[2,32,8,8192]{3,2,1,0:T(8,128)} %get-tuple-element.311, f32[2,32,8]{2,1,0:T(8,128)S(1)} %get-tuple-element.310, pred[32,8192]{1,0:T(8,128)(4,1)S(1)} %broadcast_compare_fusion), kind=kLoop, calls=%fused_computation.35 | loop fusion | flops 12582400 | bytes 17043456 | tf_op jit(solution)/shard_map/reduce_sum | solution.py:102
  334.8 13.1 %all-gather.1 = f32[8,32,8]{1,2,0:T(8,128)S(1)} all-gather(f32[2,32,8]{1,2,0:T(8,128)S(1)} %copy.110), channel_id=3, replica_groups=mesh['groups'=2,'ctx'=4,'head'=2,'rows'=2] {'ctx'}, dimensions={0}, use_global_device_ids=true | all-gather | bytes 10240 | tf_op jit(solution)/shard_map/all_gather | solution.py:19
  348.0 13.1 %all-gather = f32[8,32,8]{1,2,0:T(8,128)S(1)} all-gather(f32[2,32,8]{1,2,0:T(8,128)S(1)} %copy.109), channel_id=2, replica_groups=mesh['groups'=2,'ctx'=4,'head'=2,'rows'=2] {'ctx'}, dimensions={0}, use_global_device_ids=true | all-gather | bytes 10240 | tf_op jit(solution)/shard_map/all_gather | solution.py:19
  361.4 8.4 %fusion.20 = f32[2,8192]{1,0:T(2,128)S(1)} fusion(f32[2,32,8,8192]{3,2,1,0:T(8,128)} %get-tuple-element.311, f32[2,32,8]{2,1,0:T(8,128)S(1)} %copy.112, f32[2,32,8]{2,1,0:T(8,128)S(1)} %copy.111, pred[32,8192]{1,0:T(8,128)(4,1)S(1)} %broadcast_compare_fusion), kind=kLoop, calls=%fused_computation.37 | loop fusion | flops 16760832 | bytes 17108992 | tf_op jit(solution)/shard_map/reduce_sum | solution.py:106
  370.4 0.8 copy.146
  371.2 1.3 divide_convert_fusion
  372.6 0.8 convert_element_type.23
  (107 shorter events, 4.5 us)
Async XLA Ops:
  7.2 1.8 copy-start
  7.2 363.2 %reduce-scatter.7.cloned.1.call-start = ((), (), s32[]{:S(2)}) async-start(), calls=%async_computation.3 | async-start | bytes 81920
  8.9 17.2 %copy-start.11 = (s32[1024]{0:T(1024)}, s32[1024]{0:T(1024)S(1)}, u32[]{:S(2)}) copy-start(s32[1024]{0:T(1024)S(1)} %pad_clamp_fusion) | copy-start | bytes 12292
  13.4 12.7 %copy-start.8 = (bf16[64,4,512]{2,1,0:T(4,128)(2,1)S(1)}, bf16[64,4,512]{2,1,0:T(4,128)(2,1)}, u32[]{:S(2)}) copy-start(bf16[64,4,512]{2,1,0:T(4,128)(2,1)} %param.17) | copy-start | bytes 786436
  13.4 13.4 %copy-start.6 = (bf16[32,4,4,8,128]{4,3,2,1,0:T(8,128)(2,1)S(1)}, bf16[32,4,4,8,128]{4,3,2,1,0:T(8,128)(2,1)}, u32[]{:S(2)}) copy-start(bf16[32,4,4,8,128]{4,3,2,1,0:T(8,128)(2,1)} %reshape_reshape.11) | copy-start | bytes 3145732
  13.4 19.9 %slice-start = ((bf16[8192,512]{1,0:T(8,128)(2,1)}), bf16[32,512]{1,0:T(8,128)(2,1)S(1)}, s32[]{:S(2)}) async-start(bf16[8192,512]{1,0:T(8,128)(2,1)} %param.12), calls=%async_computation.4 | async-start | bytes 65536 | tf_op jit(solution)/shard_map/slice | solution.py:145
  26.1 9.6 %copy-start.12 = (s32[4,20]{1,0:T(4,128)S(1)}, s32[4,20]{1,0:T(4,128)}, u32[]{:S(2)}) copy-start(s32[4,20]{1,0:T(4,128)} %param.15) | copy-start | bytes 964
  26.1 9.6 %copy-start.13 = (pred[4,4]{1,0:T(4,128)(4,1)}, pred[4,4]{1,0:T(4,128)(4,1)S(1)}, u32[]{:S(2)}) copy-start(pred[4,4]{1,0:T(4,128)(4,1)S(1)} %fusion.50) | copy-start | bytes 52
  32.6 16.1 %copy-start.3 = (f32[32,4,4,8]{3,1,2,0:T(4,128)}, f32[32,4,4,8]{3,1,2,0:T(4,128)S(1)}, u32[]{:S(2)}) copy-start(f32[32,4,4,8]{3,1,2,0:T(4,128)S(1)} %get-tuple-element.312) | copy-start | bytes 49156
  48.7 199.1 %copy-start.7 = (f32[128,4,8]{0,2,1:T(8,128)S(1)}, f32[128,4,8]{0,2,1:T(8,128)}, u32[]{:S(2)}) copy-start(f32[128,4,8]{0,2,1:T(8,128)} %copy.124) | copy-start | bytes 49156
  48.7 199.1 %copy-start.9 = (f32[128,4,8]{0,2,1:T(8,128)S(1)}, f32[128,4,8]{0,2,1:T(8,128)}, u32[]{:S(2)}) copy-start(f32[128,4,8]{0,2,1:T(8,128)} %get-tuple-element.314) | copy-start | bytes 49156
  48.7 219.7 %copy-start.4 = (f32[32,4,4,8]{3,1,2,0:T(4,128)S(1)}, f32[32,4,4,8]{3,1,2,0:T(4,128)}, u32[]{:S(2)}) copy-start(f32[32,4,4,8]{3,1,2,0:T(4,128)} %copy-done.3) | copy-start | bytes 49156
  48.7 219.7 %copy-start.14 = (pred[4,4]{1,0:T(4,128)(4,1)S(1)}, pred[4,4]{1,0:T(4,128)(4,1)}, u32[]{:S(2)}) copy-start(pred[4,4]{1,0:T(4,128)(4,1)} %copy-done.13) | copy-start | bytes 52
  64.9 15.3 %copy-start.2 = (bf16[1,2048,4,128]{3,2,1,0:T(4,128)(2,1)S(1)}, bf16[1,2048,4,128]{3,2,1,0:T(4,128)(2,1)}, u32[]{:S(2)}) copy-start(bf16[1,2048,4,128]{3,2,1,0:T(4,128)(2,1)} %get-tuple-element.410) | copy-start | bytes 6291460 | tf_op jit(solution)/shard_map/while
  114.5 15.3 %copy-start.2 = (bf16[1,2048,4,128]{3,2,1,0:T(4,128)(2,1)S(1)}, bf16[1,2048,4,128]{3,2,1,0:T(4,128)(2,1)}, u32[]{:S(2)}) copy-start(bf16[1,2048,4,128]{3,2,1,0:T(4,128)(2,1)} %get-tuple-element.410) | copy-start | bytes 6291460 | tf_op jit(solution)/shard_map/while
  164.3 15.3 %copy-start.2 = (bf16[1,2048,4,128]{3,2,1,0:T(4,128)(2,1)S(1)}, bf16[1,2048,4,128]{3,2,1,0:T(4,128)(2,1)}, u32[]{:S(2)}) copy-start(bf16[1,2048,4,128]{3,2,1,0:T(4,128)(2,1)} %get-tuple-element.410) | copy-start | bytes 6291460 | tf_op jit(solution)/shard_map/while
  214.1 15.3 %copy-start.2 = (bf16[1,2048,4,128]{3,2,1,0:T(4,128)(2,1)S(1)}, bf16[1,2048,4,128]{3,2,1,0:T(4,128)(2,1)}, u32[]{:S(2)}) copy-start(bf16[1,2048,4,128]{3,2,1,0:T(4,128)(2,1)} %get-tuple-element.410) | copy-start | bytes 6291460 | tf_op jit(solution)/shard_map/while
  247.8 33.8 %slice-start.1 = ((bf16[8192,512]{1,0:T(8,128)(2,1)}), bf16[32,512]{1,0:T(8,128)(2,1)S(1)}, s32[]{:S(2)}) async-start(bf16[8192,512]{1,0:T(8,128)(2,1)} %param.13), calls=%async_computation.5 | async-start | bytes 65536 | tf_op jit(solution)/shard_map/slice | solution.py:146
  247.8 33.8 %copy-start.5 = (f32[128,4,8,32]{0,3,2,1:T(8,128)S(1)}, f32[128,4,8,32]{0,3,2,1:T(8,128)}, u32[]{:S(2)}) copy-start(f32[128,4,8,32]{0,3,2,1:T(8,128)} %get-tuple-element.315) | copy-start | bytes 1572868
  272.8 98.4 %reduce-scatter.5.cloned.1.call-start = ((), (), s32[]{:S(2)}) async-start(), calls=%async_computation.2 | async-start | bytes 2621440 | tf_op jit(solution)/shard_map/reduce_scatter | solution.py:180
  289.7 11.3 %copy-start.10 = (bf16[8,4096]{1,0:T(8,128)(2,1)S(1)}, bf16[8,4096]{1,0:T(8,128)(2,1)}, u32[]{:S(2)}) copy-start(bf16[8,4096]{1,0:T(8,128)(2,1)} %param.14) | copy-start | bytes 196612
  361.3 12.0 %copy-start.1 = (bf16[64,4,4096]{2,1,0:T(4,128)(2,1)S(1)}, bf16[64,4,4096]{2,1,0:T(4,128)(2,1)}, u32[]{:S(2)}) copy-start(bf16[64,4,4096]{2,1,0:T(4,128)(2,1)} %param.16) | copy-start | bytes 6291460
Sparse Core Ops, SparseCore 0:
  273.0 17.4 reduce-scatter.6
  292.8 43.9 reduce-scatter.4
where the time goes:
time: 382 us; the launch traced here: 380 us
  matrix products  139 us (36%)
  other arithmetic  83.7 us (22%)
  local copies, waits for them, and re-layouts  81 us (21%)
  blocking collectives  61.6 us (16%)
  between operations  14.4 us (4%)
    dot_general x5, matrix products, advance(): jnp.einsum(value_form, weights.astype(jnp.bfloat16), value_block, preferr...  70.5 us
    reduce_sum x5, other arithmetic, advance(): totals = state_now[1] * shrink + jnp.sum(weights, axis=3)  62.3 us
    dot_general x5, matrix products, advance(): jnp.einsum(score_form, queries, key_block, preferred_element_type=jnp.flo...  50.4 us
    dynamic_slice x8, local copies, waits for them, and re-layouts, fold_keys(): lax.scan(advance, start_state, (key_blocks, value_blocks, mask_blocks))  26.8 us
    all_gather x2, blocking collectives, merged(): everything = jax.tree.map(lambda part: lax.all_gather(part, axis), x)  26.3 us
    pmax x1, blocking collectives, local(): maxima = lax.pmax(partial_value[0], 'ctx')  20.6 us
    all_gather x1, blocking collectives, local(): whole_query = lax.all_gather(mine_query, 'ctx', axis=0, tiled=True)  14.7 us
    unnamed x33, local copies, waits for them, and re-layouts  13.4 us
  transfers between devices with their start and end apart: 2, of which 0 were waited for; matrix products, arithmetic and copies ran while one was open for 15% of the time, Pallas kernels for 0%

commit v1 on v0

v1 whole, which is shorter than its diff:
```python
import functools
import math

import jax
import jax.numpy as jnp
from jax import lax
from jax.experimental import pallas as pl
from jax.experimental.pallas import tpu as pltpu
from jax.sharding import PartitionSpec as P

QH = 64
KVH = 8
HD = 128
STRETCH = 512
W = 32
GROUP = QH // KVH

FILL = -1.0e30
SCALE2 = HD ** (-0.5) * math.log2(math.e)
NT = (((1,), (1,)), ((), ()))


def lanes_of(column):
    rows = []
    step = min(128, column.shape[0])
    for at in range(0, column.shape[0], step):
        block = column[at : at + step]
        eye = lax.broadcasted_iota(jnp.int32, block.shape, 0) == lax.broadcasted_iota(
            jnp.int32, block.shape, 1
        )
        rows.append(jnp.sum(jnp.where(eye, block, 0.0), axis=0, keepdims=True))
    return rows


def decode_kernel(
    heads,
    ctx_count,
    row_count,
    keep_ref,
    order_ref,
    place_ref,
    q_hbm,
    k_hbm,
    v_hbm,
    own_k_hbm,
    own_v_hbm,
    *rest,
):
    outs = rest[:ctx_count]
    (q_buf, k_buf, v_buf, kx_buf, vx_buf, m_ref, l_ref, acc_ref, q_sem, k_sem, v_sem, x_sem) = rest[
        ctx_count:
    ]
    keep_count = keep_ref.shape[1]
    here = k_hbm.shape[0] // STRETCH
    own_index = place_ref[0]
    row_index = place_ref[1]
    is_last = own_index == ctx_count - 1
    base = own_index * here
    rows_total = q_hbm.shape[0]
    rows_each = rows_total // (ctx_count * row_count)
    per_row = q_hbm.shape[2]
    local_rows = rows_each * ctx_count
    queries = local_rows * per_row
    chunk = min(256, queries)
    steps = own_k_hbm.shape[1] // rows_total
    own_keys = own_k_hbm.shape[1]

    def row_at(j):
        k = j // rows_each
        i = lax.rem(j, rows_each)
        dest = lax.rem(own_index + k, ctx_count)
        return order_ref[dest * (row_count * rows_each) + row_index * rows_each + i]

    def q_copy(j, row):
        return pltpu.make_async_copy(
            q_hbm.at[row, pl.ds(heads[0], len(heads))], q_buf.at[:, j], q_sem.at[j]
        )

    for j in range(local_rows):
        q_copy(j, row_at(j)).start()

    starts, counts = [], []
    for h in heads:
        start = jnp.int32(0)
        count = jnp.int32(0)
        for i in range(keep_count):
            local = keep_ref[h, i] - base
            start = start + (local < 0).astype(jnp.int32)
            count = count + ((local >= 0) & (local < here)).astype(jnp.int32)
        starts.append(start)
        counts.append(count)

    def unit_copies(at, u, h):
        local = keep_ref[h, starts[at] + u] - base
        rows = pl.ds(pl.multiple_of(local * STRETCH, STRETCH), STRETCH)
        cols = pl.ds(h * HD, HD)
        slot = at * here + u
        return (
            pltpu.make_async_copy(k_hbm.at[rows, cols], k_buf.at[slot], k_sem.at[slot]),
            pltpu.make_async_copy(v_hbm.at[rows, cols], v_buf.at[slot], v_sem.at[slot]),
        )

    def extra_copies(at, h):
        tail = pl.ds(k_hbm.shape[0] - W, W)
        cols = pl.ds(h * HD, HD)
        return (
            pltpu.make_async_copy(own_k_hbm.at[h], kx_buf.at[at, pl.ds(0, own_keys)], x_sem.at[at, 0]),
            pltpu.make_async_copy(own_v_hbm.at[h], vx_buf.at[at, pl.ds(0, own_keys)], x_sem.at[at, 1]),
            pltpu.make_async_copy(k_hbm.at[tail, cols], kx_buf.at[at, pl.ds(own_keys, W)], x_sem.at[at, 2]),
            pltpu.make_async_copy(v_hbm.at[tail, cols], vx_buf.at[at, pl.ds(own_keys, W)], x_sem.at[at, 3]),
        )

    for at, h in enumerate(heads):

        @pl.loop(0, counts[at])
        def _(u):
            for copy in unit_copies(at, u, h):
                copy.start()

    @pl.when(is_last)
    def _():
        rest_rows = kx_buf.shape[1] - own_keys - W
        for at, h in enumerate(heads):
            kx_buf[at, pl.ds(own_keys + W, rest_rows)] = jnp.zeros((rest_rows, HD), jnp.bfloat16)
            vx_buf[at, pl.ds(own_keys + W, rest_rows)] = jnp.zeros((rest_rows, HD), jnp.bfloat16)
            for copy in extra_copies(at, h):
                copy.start()

    for j in range(local_rows):
        q_copy(j, 0).wait()

    def fold(at, first, keys, values, mask):
        sl = pl.ds(first, chunk)
        j0 = first // per_row
        q = q_buf[at, j0 : j0 + chunk // per_row].reshape(chunk, HD)
        s = lax.dot_general(q, keys, NT, preferred_element_type=jnp.float32) * SCALE2
        if mask is not None:
            s = jnp.where(mask, s, FILL)
        m_old = m_ref[sl]
        m_new = jnp.maximum(m_old, jnp.max(s, axis=1, keepdims=True))
        alpha = jnp.exp2(m_old - m_new)
        total = None
        parts = []
        for c in range(0, s.shape[1], HD):
            p = jnp.exp2(s[:, c : c + HD] - m_new)
            if mask is not None:
                p = jnp.where(mask[:, c : c + HD], p, 0.0)
            total = p if total is None else total + p
            parts.append(p.astype(jnp.bfloat16))
        p = jnp.concatenate(parts, axis=1)
        l_ref[sl] = l_ref[sl] * alpha + total
        acc_ref[sl] = acc_ref[sl] * alpha + jnp.dot(p, values, preferred_element_type=jnp.float32)
        m_ref[sl] = m_new

    for at, h in enumerate(heads):
        m_ref[...] = jnp.full(m_ref.shape, FILL, jnp.float32)
        l_ref[...] = jnp.zeros(l_ref.shape, jnp.float32)
        acc_ref[...] = jnp.zeros(acc_ref.shape, jnp.float32)

        @pl.loop(0, counts[at])
        def _(u):
            slot = at * here + u
            for copy in unit_copies(at, u, h):
                copy.wait()
            for first in range(0, queries, chunk):
                fold(at, first, k_buf[slot], v_buf[slot], None)

        @pl.when(is_last)
        def _():
            for copy in extra_copies(at, h):
                copy.wait()
            width = kx_buf.shape[1]
            lane = lax.broadcasted_iota(jnp.int32, (per_row, width), 1)
            q_step = lax.rem(lax.broadcasted_iota(jnp.int32, (per_row, width), 0), steps)
            causal = (lax.rem(lane, steps) <= q_step) & (lane < own_keys)
            window = (lane >= own_keys) & (lane < own_keys + W)
            key_row = lane // steps
            for first in range(0, queries, chunk):
                masks = []
                for j in range(first // per_row, (first + chunk) // per_row):
                    masks.append(jnp.where((causal & (key_row == row_at(j))) | window, 1.0, 0.0))
                mask = jnp.concatenate(masks, axis=0) > 0.5
                fold(at, first, kx_buf[at], vx_buf[at], mask)

        per_dest = queries // ctx_count
        for k in range(ctx_count):
            sl = pl.ds(k * per_dest, per_dest)
            total = jnp.sum(l_ref[sl], axis=1, keepdims=True)
            some = total > 0.0
            out = acc_ref[sl] / jnp.where(some, total, 1.0)
            lse = jnp.where(some, m_ref[sl] + jnp.log2(jnp.where(some, total, 1.0)), FILL)
            outs[k][at, pl.ds(0, per_dest)] = out.astype(jnp.bfloat16)
            lines = lanes_of(lse)
            n = len(lines)
            high = [x.astype(jnp.bfloat16).astype(jnp.float32) for x in lines]
            mid = [(x - y).astype(jnp.bfloat16).astype(jnp.float32) for x, y in zip(lines, high)]
            low = [x - y - z for x, y, z in zip(lines, high, mid)]
            block = jnp.concatenate(
                high + mid + low + [jnp.zeros((16 - 3 * n, HD), jnp.float32)], axis=0
            )
            outs[k][at, pl.ds(per_dest, 16)] = block.astype(jnp.bfloat16)


def decode(heads, ctx_count, row_count, keep, order, place, q, keys, values, own_k, own_v):
    rows_total, _, per_row, _ = q.shape
    local_rows = rows_total // row_count
    queries = local_rows * per_row
    per_dest = queries // ctx_count
    here = keys.shape[0] // STRETCH
    width = pl.cdiv(own_k.shape[1] + W, HD) * HD
    n = len(heads)
    slots = n * here
    any_space = pl.BlockSpec(memory_space=pl.ANY)
    return pl.pallas_call(
        functools.partial(decode_kernel, heads, ctx_count, row_count),
        out_shape=[jax.ShapeDtypeStruct((n, per_dest + 16, HD), jnp.bfloat16)] * ctx_count,
        grid_spec=pltpu.PrefetchScalarGridSpec(
            num_scalar_prefetch=3,
            grid=(),
            in_specs=[any_space] * 5,
            out_specs=[pl.BlockSpec(memory_space=pltpu.VMEM)] * ctx_count,
            scratch_shapes=[
                pltpu.VMEM((n, local_rows, per_row, HD), jnp.bfloat16),
                pltpu.VMEM((slots, STRETCH, HD), jnp.bfloat16),
                pltpu.VMEM((slots, STRETCH, HD), jnp.bfloat16),
                pltpu.VMEM((n, width, HD), jnp.bfloat16),
                pltpu.VMEM((n, width, HD), jnp.bfloat16),
                pltpu.VMEM((queries, HD), jnp.float32),
                pltpu.VMEM((queries, HD), jnp.float32),
                pltpu.VMEM((queries, HD), jnp.float32),
                pltpu.SemaphoreType.DMA((local_rows,)),
                pltpu.SemaphoreType.DMA((slots,)),
                pltpu.SemaphoreType.DMA((slots,)),
                pltpu.SemaphoreType.DMA((n, 4)),
            ],
        ),
        cost_estimate=pl.CostEstimate(
            flops=n * 8 * queries * STRETCH * HD * 4,
            bytes_accessed=n * 8 * STRETCH * HD * 4,
            transcendentals=n * 8 * queries * STRETCH,
        ),
        name="decode",
    )(keep, order, place, q, keys, values, own_k, own_v)


def window_kernel(ctx_count, place_ref, q_ref, k_ref, max_ref, sum_ref):
    block = pl.program_id(1)
    own_index = place_ref[0]
    q = q_ref[...].reshape(-1, HD)
    per_piece = q.shape[0] // ctx_count
    w_each = W // ctx_count
    count = k_ref.shape[0] // STRETCH
    last_block = (own_index == ctx_count - 1) & (block == pl.num_programs(1) - 1)
    row = lax.broadcasted_iota(jnp.int32, (W, q.shape[0]), 0)
    col = lax.broadcasted_iota(jnp.int32, (W, q.shape[0]), 1)
    w = (ctx_count - 1 - col // per_piece) * w_each + lax.rem(col, w_each)
    allowed = (row <= w) | jnp.logical_not(last_block)
    for c in range(count):
        keys = k_ref[pl.ds(c * STRETCH, STRETCH)]
        s = lax.dot_general(keys, q, NT, preferred_element_type=jnp.float32) * SCALE2
        if c == count - 1:
            s = jnp.concatenate([s[: STRETCH - W], jnp.where(allowed, s[STRETCH - W :], FILL)], axis=0)
        peak = jnp.max(s, axis=0, keepdims=True)
        max_ref[0, pl.ds(c, 1)] = peak
        sum_ref[0, pl.ds(c, 1)] = jnp.sum(jnp.exp2(s - peak), axis=0, keepdims=True)


def window(ctx_count, score_heads, place, pieces, keys):
    here = keys.shape[0] // STRETCH
    per_block = math.gcd(here, 8)
    queries = W * GROUP
    stats = jax.ShapeDtypeStruct((score_heads, here, queries), jnp.float32)
    return pl.pallas_call(
        functools.partial(window_kernel, ctx_count),
        out_shape=[stats, stats],
        grid_spec=pltpu.PrefetchScalarGridSpec(
            num_scalar_prefetch=1,
            grid=(score_heads, here // per_block),
            in_specs=[
                pl.BlockSpec(
                    (ctx_count, 1, queries // ctx_count, HD), lambda g, b, place: (0, g, 0, 0)
                ),
                pl.BlockSpec(
                    (per_block * STRETCH, HD), lambda g, b, place: (b, place[1] * score_heads + g)
                ),
            ],
            out_specs=[
                pl.BlockSpec((1, per_block, queries), lambda g, b, place: (g, b, 0)),
                pl.BlockSpec((1, per_block, queries), lambda g, b, place: (g, b, 0)),
            ],
        ),
        cost_estimate=pl.CostEstimate(
            flops=score_heads * queries * keys.shape[0] * HD * 2,
            bytes_accessed=score_heads * keys.shape[0] * HD * 2,
            transcendentals=score_heads * queries * keys.shape[0],
        ),
        name="window",
    )(place, pieces, keys)


def combine_kernel(ctx_count, groups, *refs):
    out_ref = refs[-1]
    for at_group, heads in enumerate(groups):
        parts = refs[at_group * ctx_count : (at_group + 1) * ctx_count]
        per_dest = parts[0].shape[1] - 16
        step = min(128, per_dest)
        n = per_dest // step
        for at, h in enumerate(heads):
            for b in range(n):
                lses = []
                for part in parts:
                    tail = part[at, pl.ds(per_dest, 16)].astype(jnp.float32)
                    line = tail[b : b + 1] + tail[n + b : n + b + 1] + tail[2 * n + b : 2 * n + b + 1]
                    lses.append(line)
                top = functools.reduce(jnp.maximum, lses)
                weights = [jnp.exp2(x - top) for x in lses]
                whole = functools.reduce(jnp.add, weights)
                total = None
                for part, weight in zip(parts, weights):
                    share = jnp.broadcast_to(weight / whole, (128, HD)).T[:step]
                    term = part[at, pl.ds(b * step, step)].astype(jnp.float32) * share
                    total = term if total is None else total + term
                per_row = GROUP * 4
                lines = step // per_row
                out_ref[pl.ds(b * lines, lines), h] = total.reshape(lines, per_row, HD).astype(
                    jnp.bfloat16
                )


def local(keys, values, window_q, keep_stretches, dec_q, dec_k, dec_v, row_order):
    ctx_count = lax.axis_size("ctx")
    row_count = lax.axis_size("rows")
    own_index = lax.axis_index("ctx")
    row_index = lax.axis_index("rows")
    place = jnp.stack([own_index, row_index]).astype(jnp.int32)
    heads = keys.shape[1] // HD
    rows_total, steps = dec_q.shape[:2]
    score_heads = heads // row_count
    shifts = range(1, ctx_count)

    def shifted(x, k):
        return lax.ppermute(x, "ctx", [(i, (i + k) % ctx_count) for i in range(ctx_count)])

    w_each = window_q.shape[0]
    window_tiles = window_q.reshape(w_each, heads * GROUP, HD).transpose(1, 0, 2)
    window_tiles = window_tiles.reshape(heads, GROUP * w_each, HD)
    mine = lax.dynamic_slice_in_dim(window_tiles, row_index * score_heads, score_heads, 0)
    pieces = jnp.stack([mine] + [shifted(mine, k) for k in shifts])

    q = dec_q.reshape(rows_total, steps, heads * GROUP, HD).transpose(0, 2, 1, 3)
    q = q.reshape(rows_total, heads, GROUP * steps, HD)
    own_k = dec_k.reshape(rows_total, steps, heads, HD).transpose(2, 0, 1, 3)
    own_k = own_k.reshape(heads, rows_total * steps, HD)
    own_v = dec_v.reshape(rows_total, steps, heads, HD).transpose(2, 0, 1, 3)
    own_v = own_v.reshape(heads, rows_total * steps, HD)

    groups = [tuple([h]) for h in range(heads)]
    operands = []
    for group in groups:
        parts = decode(
            group, ctx_count, row_count, keep_stretches, row_order, place, q, keys, values, own_k, own_v
        )
        operands += [parts[0]] + [shifted(parts[k], k) for k in shifts]

    peaks, sums = window(ctx_count, score_heads, place, pieces, keys)
    top = jnp.max(peaks, axis=1)
    total = jnp.sum(sums * jnp.exp2(peaks - top[:, None]), axis=1)
    stat = jnp.stack([top, total]).reshape(2, score_heads, ctx_count, -1)
    stats = [stat] + [jnp.roll(shifted(stat, k), k, axis=2) for k in shifts]
    tops = jnp.stack([x[0] for x in stats])
    peak = jnp.max(tops, axis=0)
    whole = sum(x[1] * jnp.exp2(x[0] - peak) for x in stats)
    peak, whole = peak.reshape(score_heads, -1), whole.reshape(score_heads, -1)
    stretch_scores = jnp.sum(sums * (jnp.exp2(peaks - peak[:, None]) / whole[:, None]), axis=2)

    rows_each = rows_total // (ctx_count * row_count)
    decoded = pl.pallas_call(
        functools.partial(combine_kernel, ctx_count, groups),
        out_shape=jax.ShapeDtypeStruct((rows_each, heads, GROUP * steps, HD), jnp.bfloat16),
        in_specs=[pl.BlockSpec(memory_space=pltpu.VMEM)] * len(operands),
        out_specs=pl.BlockSpec(memory_space=pltpu.VMEM),
        name="combine",
    )(*operands)
    decoded = decoded.reshape(rows_each, heads * GROUP, steps, HD).transpose(0, 2, 1, 3)
    return (stretch_scores, decoded.reshape(rows_each, steps, heads * GROUP * HD))


def solution(mesh):
    placed = (
        P(("groups", "ctx"), "head"),
        P(("groups", "ctx"), "head"),
        P(("groups", "ctx"), "head"),
        P(("groups", "head"), None),
        P("groups", None, "head"),
        P("groups", None, "head"),
        P("groups", None, "head"),
        P("groups"),
    )
    return jax.shard_map(
        local,
        mesh=mesh,
        in_specs=placed,
        out_specs=(
            P(("groups", "head", "rows"), "ctx"),
            P(("groups", "ctx", "rows"), None, "head"),
        ),
        check_vma=False,
    )
```

time: 382 us -> 163 us (0.43)
  matrix products: 139 us -> 0 us
  Pallas kernels: 0 us -> 93.2 us
  other arithmetic: 83.7 us -> 3.61 us
  local copies, waits for them, and re-layouts: 81 us -> 4.67 us
  blocking collectives: 61.6 us -> 0 us
  starting transfers between devices: 0.08 us -> 48.3 us
  waiting for transfers between devices: 0.04 us -> 13.5 us
  between operations: 14.4 us -> 1 us
    dot_general x13 -> x0, matrix products: 139 us -> none  [the longest x5 70.5 us: advance(): jnp.einsum(value_form, weights.astype(jnp.bfloat16), value_block, preferr...]
    pallas_call x0 -> x6, Pallas kernels: none -> 93.2 us  [the longest x4 82.9 us: decode(): pl.pallas_call(functools.partial(decode_kernel, heads, ctx_count, row_cou...]
    reduce_sum x10 -> x2, other arithmetic: 82 us -> 1.47 us  [the longest x1 0.8 us: local(): total = jnp.sum(sums * jnp.exp2(peaks - top[:, None]), axis=1)]
    ppermute x0 -> x18, starting transfers between devices: none -> 48.3 us  [shifted(): lax.ppermute(x, 'ctx', [(i, (i + k) % ctx_count) for i in range(ctx_count)])]
    all_gather x3 -> x0, blocking collectives: 41 us -> none  [the longest x2 26.3 us: merged(): everything = jax.tree.map(lambda part: lax.all_gather(part, axis), x)]
    another operation x3 -> x4, local copies, waits for them, and re-layouts: 27.1 us -> 0.19 us  [the longest x3 0.18 us: local(): stat = jnp.stack([top, total]).reshape(2, score_heads, ctx_count, -1)]
    dynamic_slice x9 -> x1, local copies, waits for them, and re-layouts: 26.8 us -> 0.8 us  [local(): lax.dynamic_slice_in_dim(window_tiles, row_index * score_heads, score_hea...]
    pmax x1 -> x0, blocking collectives: 20.6 us -> none  [local(): maxima = lax.pmax(partial_value[0], 'ctx')]
  transfers between devices with their start and end apart: 2 -> 18, of which waited for: 0 -> 6; matrix products, arithmetic and copies ran while one was open for 15% -> 4% of each run, Pallas kernels for 0% -> 55%
where the time goes in v1:
time: 163 us; the launch traced here: 164 us
  Pallas kernels  93.2 us (57%)
  starting transfers between devices  48.3 us (30%)
  waiting for transfers between devices  13.5 us (8%)
  local copies, waits for them, and re-layouts  4.67 us (3%)
  other arithmetic  3.61 us (2%)
    pallas_call x4, Pallas kernels, decode(): pl.pallas_call(functools.partial(decode_kernel, heads, ctx_count, row_cou...  82.9 us
    ppermute x18, starting transfers between devices, shifted(): lax.ppermute(x, 'ctx', [(i, (i + k) % ctx_count) for i in range(ctx_count)])  48.3 us
    ppermute x18, waiting for transfers between devices, shifted(): lax.ppermute(x, 'ctx', [(i, (i + k) % ctx_count) for i in range(ctx_count)])  13.5 us
    pallas_call x1, Pallas kernels, window(): pl.pallas_call(functools.partial(window_kernel, ctx_count), out_shape=[st...  7.72 us
  transfers between devices with their start and end apart: 18, of which 6 were waited for; matrix products, arithmetic and copies ran while one was open for 4% of the time, Pallas kernels for 55%

profile of v1, /device:TPU:0, one launch (start us, length us, event | category | flops | bytes accessed | tf_op | source)
XLA Modules:
  0.0 164.3 jit_solution(12355747758379522224)
XLA Ops:
  0.6 0.0 copy-start
  0.7 0.8 constant_dynamic-slice_fusion
  1.5 3.1 %collective-permute-start = (bf16[2,64,128]{2,1,0:T(8,128)(2,1)S(1)}, bf16[2,64,128]{2,1,0:T(8,128)(2,1)S(1)}, u32[]{:S(2)}, u32[]{:S(2)}) collective-permute-start(bf16[2,64,128]{2,1,0:T(8,128)(2,1)S(1)} %constant_dynamic-slice_fusion), channel_id=1, source_target_pairs={{0,4},{4,8},{8,12},{12,0},{1,5},{5,9},{9,13},{13,1},{2,6},{6,10},{... | collective-permute-start | bytes 98312 | tf_op jit(solution)/shard_map/ppermute | solution.py:342
  4.5 2.6 %collective-permute-start.1 = (bf16[2,64,128]{2,1,0:T(8,128)(2,1)S(1)}, bf16[2,64,128]{2,1,0:T(8,128)(2,1)S(1)}, u32[]{:S(2)}, u32[]{:S(2)}) collective-permute-start(bf16[2,64,128]{2,1,0:T(8,128)(2,1)S(1)} %constant_dynamic-slice_fusion), channel_id=1, source_target_pairs={{0,8},{4,12},{8,0},{12,4},{1,9},{5,13},{9,1},{13,5},{2,10},{6,14},... | collective-permute-start | bytes 98312 | tf_op jit(solution)/shard_map/ppermute | solution.py:342
  7.1 1.3 collective-permute-start.2
  8.4 0.8 copy_bitcast_fusion.1
  9.2 1.8 %copy_bitcast_fusion = bf16[64,4,4,128]{3,1,0,2:T(4,128)(2,1)} fusion(bf16[64,4,512]{2,1,0:T(4,128)(2,1)} %param.14), kind=kLoop, calls=%fused_computation | loop fusion | bytes 524288 | tf_op jit(solution)/shard_map/reshape | solution.py:354
  11.0 0.6 pad_add_fusion.place_ref
  11.6 3.4 %decode.5 = (bf16[1,272,128]{2,1,0:T(8,128)(2,1)}, bf16[1,272,128]{2,1,0:T(8,128)(2,1)}, bf16[1,272,128]{2,1,0:T(8,128)(2,1)}, bf16[1,272,128]{2,1,0:T(8,128)(2,1)}) custom-call(s32[4,20]{1,0:T(4,128)} %keep_ref.7, s32[64]{0:T(128)} %order_ref.7, s32[2]{0:T(128)} %pad_add_fusion.place_ref, bf16[64,4,32,128]{3,2,1,0:T(8,128)(2,1)} %bitcast.39, ...), custom_call_target="tpu_custom_call" | custom-call | flops 2147483648 | bytes 2097152 | tf_op jit(solution)/shard_map/decode/pallas_call | solution.py:214
  15.0 0.2 collective-permute-start.10
  15.2 26.0 %collective-permute-start.11 = (bf16[1,272,128]{2,1,0:T(8,128)(2,1)}, bf16[1,272,128]{2,1,0:T(8,128)(2,1)S(1)}, u32[]{:S(2)}, u32[]{:S(2)}) collective-permute-start(bf16[1,272,128]{2,1,0:T(8,128)(2,1)} %get-tuple-element.29), channel_id=1, source_target_pairs={{0,12},{4,0},{8,4},{12,8},{1,13},{5,1},{9,5},{13,9},{2,14},{6,2},{... | collective-permute-start | bytes 208904 | tf_op jit(solution)/shard_map/ppermute | solution.py:342
  41.2 26.5 %decode.6 = (bf16[1,272,128]{2,1,0:T(8,128)(2,1)}, bf16[1,272,128]{2,1,0:T(8,128)(2,1)}, bf16[1,272,128]{2,1,0:T(8,128)(2,1)}, bf16[1,272,128]{2,1,0:T(8,128)(2,1)}) custom-call(s32[4,20]{1,0:T(4,128)} %keep_ref.7, s32[64]{0:T(128)} %order_ref.7, s32[2]{0:T(128)} %pad_add_fusion.place_ref, bf16[64,4,32,128]{3,2,1,0:T(8,128)(2,1)} %bitcast.40, ...), custom_call_target="tpu_custom_call" | custom-call | flops 2147483648 | bytes 2097152 | tf_op jit(solution)/shard_map/decode/pallas_call | solution.py:214
  67.7 0.0 copy-start.15
  67.7 26.6 %decode.7 = (bf16[1,272,128]{2,1,0:T(8,128)(2,1)}, bf16[1,272,128]{2,1,0:T(8,128)(2,1)}, bf16[1,272,128]{2,1,0:T(8,128)(2,1)}, bf16[1,272,128]{2,1,0:T(8,128)(2,1)}) custom-call(s32[4,20]{1,0:T(4,128)} %keep_ref.7, s32[64]{0:T(128)} %order_ref.7, s32[2]{0:T(128)} %pad_add_fusion.place_ref, bf16[64,4,32,128]{3,2,1,0:T(8,128)(2,1)} %bitcast.41, ...), custom_call_target="tpu_custom_call" | custom-call | flops 2147483648 | bytes 2097152 | tf_op jit(solution)/shard_map/decode/pallas_call | solution.py:214
  94.3 0.1 collective-permute-start.12
  94.4 0.1 collective-permute-start.13
  94.5 0.7 pad_maximum_fusion.q_ref
  95.2 7.7 %window.1 = (f32[2,16,256]{2,1,0:T(8,128)}, f32[2,16,256]{2,1,0:T(8,128)}) custom-call(s32[2]{0:T(128)} %pad_add_fusion.place_ref, bf16[4,2,64,128]{3,2,1,0:T(8,128)(2,1)} %pad_maximum_fusion.q_ref, bf16[8192,512]{1,0:T(8,128)(2,1)} %k_hbm.7), custom_call_target="tpu_custom_call" | custom-call | flops 1073741824 | bytes 4194304 | tf_op jit(solution)/shard_map/window/pallas_call | solution.py:273
  102.9 0.8 reduce_max.49
  103.7 0.1 stack.42
  103.8 0.8 multiply_reduce_fusion.1
  104.6 0.1 stack.43
  104.7 4.3 %collective-permute-start.3 = (f32[2,2,4,64]{3,2,1,0:T(4,128)S(1)}, f32[2,2,4,64]{3,2,1,0:T(4,128)S(1)}, u32[]{:S(2)}, u32[]{:S(2)}) collective-permute-start(f32[2,2,4,64]{3,2,1,0:T(4,128)S(1)} %constant_dynamic-update-slice_fusion), channel_id=1, source_target_pairs={{0,4},{4,8},{8,12},{12,0},{1,5},{5,9},{9,13},{13,1},{2,6},{6,10},{... | collective-permute-start | bytes 12296 | tf_op jit(solution)/shard_map/ppermute | solution.py:342
  109.0 26.5 %decode.4 = (bf16[1,272,128]{2,1,0:T(8,128)(2,1)}, bf16[1,272,128]{2,1,0:T(8,128)(2,1)}, bf16[1,272,128]{2,1,0:T(8,128)(2,1)}, bf16[1,272,128]{2,1,0:T(8,128)(2,1)}) custom-call(s32[4,20]{1,0:T(4,128)} %keep_ref.7, s32[64]{0:T(128)} %order_ref.7, s32[2]{0:T(128)} %pad_add_fusion.place_ref, bf16[64,4,32,128]{3,2,1,0:T(8,128)(2,1)} %bitcast.42, ...), custom_call_target="tpu_custom_call" | custom-call | flops 2147483648 | bytes 2097152 | tf_op jit(solution)/shard_map/decode/pallas_call | solution.py:214
  135.5 0.1 collective-permute-start.4
  135.6 4.5 %collective-permute-done.4 = f32[2,2,4,64]{3,2,1,0:T(4,128)S(1)} collective-permute-done((f32[2,2,4,64]{3,2,1,0:T(4,128)S(1)}, f32[2,2,4,64]{3,2,1,0:T(4,128)S(1)}, u32[]{:S(2)}, u32[]{:S(2)}) %collective-permute-start.4) | collective-permute-done | bytes 4128 | tf_op jit(solution)/shard_map/ppermute | solution.py:342
  140.2 0.1 reduce_max.50
  140.2 0.1 squeeze.6
  140.3 0.1 reduce_max.52
  140.4 0.1 squeeze.7
  140.5 3.3 %collective-permute-done.5 = f32[2,2,4,64]{3,2,1,0:T(4,128)S(1)} collective-permute-done((f32[2,2,4,64]{3,2,1,0:T(4,128)S(1)}, f32[2,2,4,64]{3,2,1,0:T(4,128)S(1)}, u32[]{:S(2)}, u32[]{:S(2)}) %collective-permute-start.5) | collective-permute-done | bytes 4128 | tf_op jit(solution)/shard_map/ppermute | solution.py:342
  143.8 1.8 %collective-permute-start.14 = (bf16[1,272,128]{2,1,0:T(8,128)(2,1)S(1)}, bf16[1,272,128]{2,1,0:T(8,128)(2,1)S(1)}, u32[]{:S(2)}, u32[]{:S(2)}) collective-permute-start(bf16[1,272,128]{2,1,0:T(8,128)(2,1)S(1)} %copy-done.20), channel_id=1, source_target_pairs={{0,12},{4,0},{8,4},{12,8},{1,13},{5,1},{9,5},{13,9},{2,14},{6,2},{... | collective-permute-start | bytes 208904 | tf_op jit(solution)/shard_map/ppermute | solution.py:342
  145.6 0.1 reduce_max.54
  145.7 0.1 squeeze.16
  145.8 0.2 collective-permute-start.15
  146.1 0.5 collective-permute-start.16
  146.6 3.3 %collective-permute-start.17 = (bf16[1,272,128]{2,1,0:T(8,128)(2,1)S(1)}, bf16[1,272,128]{2,1,0:T(8,128)(2,1)S(1)}, u32[]{:S(2)}, u32[]{:S(2)}) collective-permute-start(bf16[1,272,128]{2,1,0:T(8,128)(2,1)S(1)} %copy-done.17), channel_id=1, source_target_pairs={{0,12},{4,0},{8,4},{12,8},{1,13},{5,1},{9,5},{13,9},{2,14},{6,2},{... | collective-permute-start | bytes 208904 | tf_op jit(solution)/shard_map/ppermute | solution.py:342
  149.9 0.6 collective-permute-start.6
  150.5 1.5 collective-permute-start.7
  152.0 0.3 collective-permute-done.15.refs_13_
  152.2 2.6 %collective-permute-start.8 = (bf16[1,272,128]{2,1,0:T(8,128)(2,1)}, bf16[1,272,128]{2,1,0:T(8,128)(2,1)S(1)}, u32[]{:S(2)}, u32[]{:S(2)}) collective-permute-start(bf16[1,272,128]{2,1,0:T(8,128)(2,1)} %get-tuple-element.25), channel_id=1, source_target_pairs={{0,12},{4,0},{8,4},{12,8},{1,13},{5,1},{9,5},{13,9},{2,14},{6,2},{... | collective-permute-start | bytes 208904 | tf_op jit(solution)/shard_map/ppermute | solution.py:342
  154.8 0.1 collective-permute-start.9
  154.9 0.7 multiply_reduce_fusion
  155.6 0.7 collective-permute-done.6.refs_1_
  156.3 1.3 collective-permute-done.7.refs_2_
  157.6 3.4 %collective-permute-done.9.refs_5_ = bf16[1,272,128]{2,1,0:T(8,128)(2,1)S(1)} collective-permute-done((bf16[1,272,128]{2,1,0:T(8,128)(2,1)S(1)}, bf16[1,272,128]{2,1,0:T(8,128)(2,1)S(1)}, u32[]{:S(2)}, u32[]{:S(2)}) %collective-permute-start.9) | collective-permute-done | bytes 69664 | tf_op jit(solution)/shard_map/ppermute | solution.py:342
  161.1 0.5 copy-done.14
  161.6 2.6 %combine.1 = bf16[8,4,32,128]{3,2,1,0:T(8,128)(2,1)} custom-call(bf16[1,272,128]{2,1,0:T(8,128)(2,1)} %get-tuple-element.22.refs_0_, bf16[1,272,128]{2,1,0:T(8,128)(2,1)} %copy-done.11, bf16[1,272,128]{2,1,0:T(8,128)(2,1)} %copy-done.12, bf16[1,272,128]{2,1,0:T(8,128)(2,1)} %copy-done.13, bf16[1,272,128]{2,1,0:T(8,128)(2,1)} %get-tuple-element.26.refs_4_, ...), custom_call_target="tpu_custom_call" | custom-call | tf_op jit(solution)/shard_map/combine/pallas_call | solution.py:377
  (67 shorter events, 0.2 us)
Async XLA Ops:
  0.6 7.8 %copy-start = (bf16[64,4,512]{2,1,0:T(4,128)(2,1)S(1)}, bf16[64,4,512]{2,1,0:T(4,128)(2,1)}, u32[]{:S(2)}) copy-start(bf16[64,4,512]{2,1,0:T(4,128)(2,1)} %param.13) | copy-start | bytes 786436
  1.5 92.9 %collective-permute-start = (bf16[2,64,128]{2,1,0:T(8,128)(2,1)S(1)}, bf16[2,64,128]{2,1,0:T(8,128)(2,1)S(1)}, u32[]{:S(2)}, u32[]{:S(2)}) collective-permute-start(bf16[2,64,128]{2,1,0:T(8,128)(2,1)S(1)} %constant_dynamic-slice_fusion), channel_id=1, source_target_pairs={{0,4},{4,8},{8,12},{12,0},{1,5},{5,9},{9,13},{13,1},{2,6},{6,10},{... | collective-permute-start | bytes 98312 | tf_op jit(solution)/shard_map/ppermute | solution.py:342
  4.5 89.9 %collective-permute-start.1 = (bf16[2,64,128]{2,1,0:T(8,128)(2,1)S(1)}, bf16[2,64,128]{2,1,0:T(8,128)(2,1)S(1)}, u32[]{:S(2)}, u32[]{:S(2)}) collective-permute-start(bf16[2,64,128]{2,1,0:T(8,128)(2,1)S(1)} %constant_dynamic-slice_fusion), channel_id=1, source_target_pairs={{0,8},{4,12},{8,0},{12,4},{1,9},{5,13},{9,1},{13,5},{2,10},{6,14},... | collective-permute-start | bytes 98312 | tf_op jit(solution)/shard_map/ppermute | solution.py:342
  7.1 87.4 %collective-permute-start.2 = (bf16[2,64,128]{2,1,0:T(8,128)(2,1)S(1)}, bf16[2,64,128]{2,1,0:T(8,128)(2,1)S(1)}, u32[]{:S(2)}, u32[]{:S(2)}) collective-permute-start(bf16[2,64,128]{2,1,0:T(8,128)(2,1)S(1)} %constant_dynamic-slice_fusion), channel_id=1, source_target_pairs={{0,12},{4,0},{8,4},{12,8},{1,13},{5,1},{9,5},{13,9},{2,14},{6,2},{... | collective-permute-start | bytes 98312 | tf_op jit(solution)/shard_map/ppermute | solution.py:342
  15.0 130.8 %collective-permute-start.10 = (bf16[1,272,128]{2,1,0:T(8,128)(2,1)}, bf16[1,272,128]{2,1,0:T(8,128)(2,1)S(1)}, u32[]{:S(2)}, u32[]{:S(2)}) collective-permute-start(bf16[1,272,128]{2,1,0:T(8,128)(2,1)} %get-tuple-element.28), channel_id=1, source_target_pairs={{0,8},{4,12},{8,0},{12,4},{1,9},{5,13},{9,1},{13,5},{2,10},{6,14},... | collective-permute-start | bytes 208904 | tf_op jit(solution)/shard_map/ppermute | solution.py:342
  15.2 130.9 %collective-permute-start.11 = (bf16[1,272,128]{2,1,0:T(8,128)(2,1)}, bf16[1,272,128]{2,1,0:T(8,128)(2,1)S(1)}, u32[]{:S(2)}, u32[]{:S(2)}) collective-permute-start(bf16[1,272,128]{2,1,0:T(8,128)(2,1)} %get-tuple-element.29), channel_id=1, source_target_pairs={{0,12},{4,0},{8,4},{12,8},{1,13},{5,1},{9,5},{13,9},{2,14},{6,2},{... | collective-permute-start | bytes 208904 | tf_op jit(solution)/shard_map/ppermute | solution.py:342
  67.7 26.6 %copy-start.15 = (bf16[8,4096]{1,0:T(8,128)(2,1)S(1)}, bf16[8,4096]{1,0:T(8,128)(2,1)}, u32[]{:S(2)}) copy-start(bf16[8,4096]{1,0:T(8,128)(2,1)} %param.10) | copy-start | bytes 196612
  67.7 26.7 %copy-start.22 = (bf16[1,272,128]{2,1,0:T(8,128)(2,1)S(1)}, bf16[1,272,128]{2,1,0:T(8,128)(2,1)}, u32[]{:S(2)}) copy-start(bf16[1,272,128]{2,1,0:T(8,128)(2,1)} %get-tuple-element.31) | copy-start | bytes 208900
  67.7 26.7 %copy-start.21 = (bf16[1,272,128]{2,1,0:T(8,128)(2,1)S(1)}, bf16[1,272,128]{2,1,0:T(8,128)(2,1)}, u32[]{:S(2)}) copy-start(bf16[1,272,128]{2,1,0:T(8,128)(2,1)} %get-tuple-element.32) | copy-start | bytes 208900
  94.3 52.2 %collective-permute-start.12 = (bf16[1,272,128]{2,1,0:T(8,128)(2,1)S(1)}, bf16[1,272,128]{2,1,0:T(8,128)(2,1)S(1)}, u32[]{:S(2)}, u32[]{:S(2)}) collective-permute-start(bf16[1,272,128]{2,1,0:T(8,128)(2,1)S(1)} %copy-done.22), channel_id=1, source_target_pairs={{0,4},{4,8},{8,12},{12,0},{1,5},{5,9},{9,13},{13,1},{2,6},{6,10},{... | collective-permute-start | bytes 208904 | tf_op jit(solution)/shard_map/ppermute | solution.py:342
  94.4 55.5 %collective-permute-start.13 = (bf16[1,272,128]{2,1,0:T(8,128)(2,1)S(1)}, bf16[1,272,128]{2,1,0:T(8,128)(2,1)S(1)}, u32[]{:S(2)}, u32[]{:S(2)}) collective-permute-start(bf16[1,272,128]{2,1,0:T(8,128)(2,1)S(1)} %copy-done.21), channel_id=1, source_target_pairs={{0,8},{4,12},{8,0},{12,4},{1,9},{5,13},{9,1},{13,5},{2,10},{6,14},... | collective-permute-start | bytes 208904 | tf_op jit(solution)/shard_map/ppermute | solution.py:342
  104.7 39.1 %copy-start.20 = (bf16[1,272,128]{2,1,0:T(8,128)(2,1)S(1)}, bf16[1,272,128]{2,1,0:T(8,128)(2,1)}, u32[]{:S(2)}) copy-start(bf16[1,272,128]{2,1,0:T(8,128)(2,1)} %get-tuple-element.33) | copy-start | bytes 208900
  104.7 41.1 %copy-start.19 = (bf16[1,272,128]{2,1,0:T(8,128)(2,1)S(1)}, bf16[1,272,128]{2,1,0:T(8,128)(2,1)}, u32[]{:S(2)}) copy-start(bf16[1,272,128]{2,1,0:T(8,128)(2,1)} %get-tuple-element.35) | copy-start | bytes 208900
  104.7 41.4 %copy-start.18 = (bf16[1,272,128]{2,1,0:T(8,128)(2,1)S(1)}, bf16[1,272,128]{2,1,0:T(8,128)(2,1)}, u32[]{:S(2)}) copy-start(bf16[1,272,128]{2,1,0:T(8,128)(2,1)} %get-tuple-element.36) | copy-start | bytes 208900
  104.7 41.9 %copy-start.17 = (bf16[1,272,128]{2,1,0:T(8,128)(2,1)S(1)}, bf16[1,272,128]{2,1,0:T(8,128)(2,1)}, u32[]{:S(2)}) copy-start(bf16[1,272,128]{2,1,0:T(8,128)(2,1)} %get-tuple-element.37) | copy-start | bytes 208900
  104.7 50.2 %copy-start.16 = (bf16[1,272,128]{2,1,0:T(8,128)(2,1)S(1)}, bf16[1,272,128]{2,1,0:T(8,128)(2,1)}, u32[]{:S(2)}) copy-start(bf16[1,272,128]{2,1,0:T(8,128)(2,1)} %get-tuple-element.27) | copy-start | bytes 208900
  104.7 50.2 %copy-start.1 = (f32[2,16,256]{2,1,0:T(8,128)S(1)}, f32[2,16,256]{2,1,0:T(8,128)}, u32[]{:S(2)}) copy-start(f32[2,16,256]{2,1,0:T(8,128)} %get-tuple-element.21) | copy-start | bytes 98308
  104.7 50.2 %copy-start.2 = (f32[2,16,256]{2,1,0:T(8,128)S(1)}, f32[2,16,256]{2,1,0:T(8,128)}, u32[]{:S(2)}) copy-start(f32[2,16,256]{2,1,0:T(8,128)} %get-tuple-element.20) | copy-start | bytes 98308
  104.7 30.8 %collective-permute-start.3 = (f32[2,2,4,64]{3,2,1,0:T(4,128)S(1)}, f32[2,2,4,64]{3,2,1,0:T(4,128)S(1)}, u32[]{:S(2)}, u32[]{:S(2)}) collective-permute-start(f32[2,2,4,64]{3,2,1,0:T(4,128)S(1)} %constant_dynamic-update-slice_fusion), channel_id=1, source_target_pairs={{0,4},{4,8},{8,12},{12,0},{1,5},{5,9},{9,13},{13,1},{2,6},{6,10},{... | collective-permute-start | bytes 12296 | tf_op jit(solution)/shard_map/ppermute | solution.py:342
  135.5 4.6 %collective-permute-start.4 = (f32[2,2,4,64]{3,2,1,0:T(4,128)S(1)}, f32[2,2,4,64]{3,2,1,0:T(4,128)S(1)}, u32[]{:S(2)}, u32[]{:S(2)}) collective-permute-start(f32[2,2,4,64]{3,2,1,0:T(4,128)S(1)} %constant_dynamic-update-slice_fusion), channel_id=1, source_target_pairs={{0,8},{4,12},{8,0},{12,4},{1,9},{5,13},{9,1},{13,5},{2,10},{6,14},... | collective-permute-start | bytes 12296 | tf_op jit(solution)/shard_map/ppermute | solution.py:342
  140.1 3.7 %collective-permute-start.5 = (f32[2,2,4,64]{3,2,1,0:T(4,128)S(1)}, f32[2,2,4,64]{3,2,1,0:T(4,128)S(1)}, u32[]{:S(2)}, u32[]{:S(2)}) collective-permute-start(f32[2,2,4,64]{3,2,1,0:T(4,128)S(1)} %constant_dynamic-update-slice_fusion), channel_id=1, source_target_pairs={{0,12},{4,0},{8,4},{12,8},{1,13},{5,1},{9,5},{13,9},{2,14},{6,2},{... | collective-permute-start | bytes 12296 | tf_op jit(solution)/shard_map/ppermute | solution.py:342
  143.8 6.7 %collective-permute-start.14 = (bf16[1,272,128]{2,1,0:T(8,128)(2,1)S(1)}, bf16[1,272,128]{2,1,0:T(8,128)(2,1)S(1)}, u32[]{:S(2)}, u32[]{:S(2)}) collective-permute-start(bf16[1,272,128]{2,1,0:T(8,128)(2,1)S(1)} %copy-done.20), channel_id=1, source_target_pairs={{0,12},{4,0},{8,4},{12,8},{1,13},{5,1},{9,5},{13,9},{2,14},{6,2},{... | collective-permute-start | bytes 208904 | tf_op jit(solution)/shard_map/ppermute | solution.py:342
  145.8 15.2 %copy-start.3 = (bf16[1,272,128]{2,1,0:T(8,128)(2,1)}, bf16[1,272,128]{2,1,0:T(8,128)(2,1)S(1)}, u32[]{:S(2)}) copy-start(bf16[1,272,128]{2,1,0:T(8,128)(2,1)S(1)} %collective-permute-done.10.refs_6_) | copy-start | bytes 208900
  145.8 6.4 %collective-permute-start.15 = (bf16[1,272,128]{2,1,0:T(8,128)(2,1)S(1)}, bf16[1,272,128]{2,1,0:T(8,128)(2,1)S(1)}, u32[]{:S(2)}, u32[]{:S(2)}) collective-permute-start(bf16[1,272,128]{2,1,0:T(8,128)(2,1)S(1)} %copy-done.19), channel_id=1, source_target_pairs={{0,4},{4,8},{8,12},{12,0},{1,5},{5,9},{9,13},{13,1},{2,6},{6,10},{... | collective-permute-start | bytes 208904 | tf_op jit(solution)/shard_map/ppermute | solution.py:342
  146.1 14.9 %copy-start.4 = (bf16[1,272,128]{2,1,0:T(8,128)(2,1)}, bf16[1,272,128]{2,1,0:T(8,128)(2,1)S(1)}, u32[]{:S(2)}) copy-start(bf16[1,272,128]{2,1,0:T(8,128)(2,1)S(1)} %collective-permute-done.11.refs_7_) | copy-start | bytes 208900
  146.1 8.8 %collective-permute-start.16 = (bf16[1,272,128]{2,1,0:T(8,128)(2,1)S(1)}, bf16[1,272,128]{2,1,0:T(8,128)(2,1)S(1)}, u32[]{:S(2)}, u32[]{:S(2)}) collective-permute-start(bf16[1,272,128]{2,1,0:T(8,128)(2,1)S(1)} %copy-done.18), channel_id=1, source_target_pairs={{0,8},{4,12},{8,0},{12,4},{1,9},{5,13},{9,1},{13,5},{2,10},{6,14},... | collective-permute-start | bytes 208904 | tf_op jit(solution)/shard_map/ppermute | solution.py:342
  146.6 14.5 %copy-start.5 = (bf16[1,272,128]{2,1,0:T(8,128)(2,1)}, bf16[1,272,128]{2,1,0:T(8,128)(2,1)S(1)}, u32[]{:S(2)}) copy-start(bf16[1,272,128]{2,1,0:T(8,128)(2,1)S(1)} %collective-permute-done.12.refs_9_) | copy-start | bytes 208900
  146.6 9.0 %collective-permute-start.17 = (bf16[1,272,128]{2,1,0:T(8,128)(2,1)S(1)}, bf16[1,272,128]{2,1,0:T(8,128)(2,1)S(1)}, u32[]{:S(2)}, u32[]{:S(2)}) collective-permute-start(bf16[1,272,128]{2,1,0:T(8,128)(2,1)S(1)} %copy-done.17), channel_id=1, source_target_pairs={{0,12},{4,0},{8,4},{12,8},{1,13},{5,1},{9,5},{13,9},{2,14},{6,2},{... | collective-permute-start | bytes 208904 | tf_op jit(solution)/shard_map/ppermute | solution.py:342
  149.9 11.1 %copy-start.6 = (bf16[1,272,128]{2,1,0:T(8,128)(2,1)}, bf16[1,272,128]{2,1,0:T(8,128)(2,1)S(1)}, u32[]{:S(2)}) copy-start(bf16[1,272,128]{2,1,0:T(8,128)(2,1)S(1)} %collective-permute-done.13.refs_10_) | copy-start | bytes 208900
  149.9 6.4 %collective-permute-start.6 = (bf16[1,272,128]{2,1,0:T(8,128)(2,1)}, bf16[1,272,128]{2,1,0:T(8,128)(2,1)S(1)}, u32[]{:S(2)}, u32[]{:S(2)}) collective-permute-start(bf16[1,272,128]{2,1,0:T(8,128)(2,1)} %get-tuple-element.23), channel_id=1, source_target_pairs={{0,4},{4,8},{8,12},{12,0},{1,5},{5,9},{9,13},{13,1},{2,6},{6,10},{... | collective-permute-start | bytes 208904 | tf_op jit(solution)/shard_map/ppermute | solution.py:342
  150.5 10.5 %copy-start.7 = (bf16[1,272,128]{2,1,0:T(8,128)(2,1)}, bf16[1,272,128]{2,1,0:T(8,128)(2,1)S(1)}, u32[]{:S(2)}) copy-start(bf16[1,272,128]{2,1,0:T(8,128)(2,1)S(1)} %collective-permute-done.14.refs_11_) | copy-start | bytes 208900
  150.5 7.1 %collective-permute-start.7 = (bf16[1,272,128]{2,1,0:T(8,128)(2,1)}, bf16[1,272,128]{2,1,0:T(8,128)(2,1)S(1)}, u32[]{:S(2)}, u32[]{:S(2)}) collective-permute-start(bf16[1,272,128]{2,1,0:T(8,128)(2,1)} %get-tuple-element.24), channel_id=1, source_target_pairs={{0,8},{4,12},{8,0},{12,4},{1,9},{5,13},{9,1},{13,5},{2,10},{6,14},... | collective-permute-start | bytes 208904 | tf_op jit(solution)/shard_map/ppermute | solution.py:342
  152.2 8.8 %copy-start.8 = (bf16[1,272,128]{2,1,0:T(8,128)(2,1)}, bf16[1,272,128]{2,1,0:T(8,128)(2,1)S(1)}, u32[]{:S(2)}) copy-start(bf16[1,272,128]{2,1,0:T(8,128)(2,1)S(1)} %collective-permute-done.15.refs_13_) | copy-start | bytes 208900
  152.2 5.4 %collective-permute-start.8 = (bf16[1,272,128]{2,1,0:T(8,128)(2,1)}, bf16[1,272,128]{2,1,0:T(8,128)(2,1)S(1)}, u32[]{:S(2)}, u32[]{:S(2)}) collective-permute-start(bf16[1,272,128]{2,1,0:T(8,128)(2,1)} %get-tuple-element.25), channel_id=1, source_target_pairs={{0,12},{4,0},{8,4},{12,8},{1,13},{5,1},{9,5},{13,9},{2,14},{6,2},{... | collective-permute-start | bytes 208904 | tf_op jit(solution)/shard_map/ppermute | solution.py:342
  154.8 6.2 %copy-start.9 = (bf16[1,272,128]{2,1,0:T(8,128)(2,1)}, bf16[1,272,128]{2,1,0:T(8,128)(2,1)S(1)}, u32[]{:S(2)}) copy-start(bf16[1,272,128]{2,1,0:T(8,128)(2,1)S(1)} %collective-permute-done.16.refs_14_) | copy-start | bytes 208900
  154.8 6.2 %collective-permute-start.9 = (bf16[1,272,128]{2,1,0:T(8,128)(2,1)S(1)}, bf16[1,272,128]{2,1,0:T(8,128)(2,1)S(1)}, u32[]{:S(2)}, u32[]{:S(2)}) collective-permute-start(bf16[1,272,128]{2,1,0:T(8,128)(2,1)S(1)} %copy-done.16), channel_id=1, source_target_pairs={{0,4},{4,8},{8,12},{12,0},{1,5},{5,9},{9,13},{13,1},{2,6},{6,10},{... | collective-permute-start | bytes 208904 | tf_op jit(solution)/shard_map/ppermute | solution.py:342
  155.6 5.5 %copy-start.10 = (bf16[1,272,128]{2,1,0:T(8,128)(2,1)}, bf16[1,272,128]{2,1,0:T(8,128)(2,1)S(1)}, u32[]{:S(2)}) copy-start(bf16[1,272,128]{2,1,0:T(8,128)(2,1)S(1)} %collective-permute-done.17.refs_15_) | copy-start | bytes 208900
  156.3 4.7 %copy-start.11 = (bf16[1,272,128]{2,1,0:T(8,128)(2,1)}, bf16[1,272,128]{2,1,0:T(8,128)(2,1)S(1)}, u32[]{:S(2)}) copy-start(bf16[1,272,128]{2,1,0:T(8,128)(2,1)S(1)} %collective-permute-done.6.refs_1_) | copy-start | bytes 208900
  157.6 3.5 %copy-start.12 = (bf16[1,272,128]{2,1,0:T(8,128)(2,1)}, bf16[1,272,128]{2,1,0:T(8,128)(2,1)S(1)}, u32[]{:S(2)}) copy-start(bf16[1,272,128]{2,1,0:T(8,128)(2,1)S(1)} %collective-permute-done.7.refs_2_) | copy-start | bytes 208900
  157.6 3.5 %copy-start.13 = (bf16[1,272,128]{2,1,0:T(8,128)(2,1)}, bf16[1,272,128]{2,1,0:T(8,128)(2,1)S(1)}, u32[]{:S(2)}) copy-start(bf16[1,272,128]{2,1,0:T(8,128)(2,1)S(1)} %collective-permute-done.8.refs_3_) | copy-start | bytes 208900
  161.0 0.6 copy-start.14
